TPU v7x, 32 devices: a whole 2x2x4 slice. The times are simulated.
32 devices in a mesh: graph: 8 (over y, x, core), dp: 4 (over z).
Axes of the slice: x: 2, y: 2, z: 4, core: 2. Of those that a mesh axis runs over, the one named last changes fastest.
Arguments:
- grid_latent: bfloat16 [4, 4096, 512], P('dp', 'graph'), may hold values from -6 to 6
- mesh_embed: bfloat16 [2048, 512], P('graph'), may hold values from -6 to 6
- mesh_edges: bfloat16 [12288, 512], P('graph'), may hold values from -6 to 6
- edge_geometry: bfloat16 [8, 4, 512], P('graph'), may hold values from -6 to 6
- edge_counts: int32 [8, 8], P('graph'), may hold values from 0 to 64, as said below
- edge_sources: int32 [8, 512], P('graph'), may hold values from 0 to 511
- edge_targets: int32 [8, 512], P('graph'), may hold values from 0 to 255
- halo_sources: int32 [8, 32], P('graph'), may hold values from 0 to 255
- mesh_sources: int32 [8, 1536], P('graph'), may hold values from 0 to 287, as said below
- mesh_targets: int32 [8, 1536], P('graph'), may hold values from 0 to 255
- grid_weight: bfloat16 [512, 512], replicated, may hold values from -0.25 to 0.25
- geometry_weight: float32 [4, 512], replicated, may hold values from -3 to 3
- message_weight: bfloat16 [512, 512], replicated, may hold values from -0.25 to 0.25
- mesh_update: bfloat16 [1024, 512], replicated, may hold values from -0.1875 to 0.1875
- mesh_output: bfloat16 [512, 512], replicated, may hold values from -0.25 to 0.25
- processor: bfloat16 [2, 3584, 512], replicated, may hold values from -0.15625 to 0.15625
- cotangent: bfloat16 [4, 2048, 512], P('dp', 'graph'), may hold values from -6 to 6
Outputs:
- mesh_result: bfloat16 [4, 2048, 512], P('dp', 'graph')
- mesh_gradient: bfloat16 [4, 2048, 512], P('dp', 'graph')
- gradients: bfloat16 [2, 3584, 512], replicated
Inputs may be any that keep to these rules, and one draw needn't show every extreme that they name: Slots of device s for device d beyond edge_counts[s, d] are empty; every device fills all 64 slots for itself, and every device fills all 64 slots for one common device. `edge_sources`: row s holds local grid rows of device s. `edge_targets`: row d holds local mesh rows of device d, for slot c from device s at column s * 64 + c. `halo_sources`: row s, columns d * 4 to d * 4 + 3 are the local rows that device s sends to device d; every device sends 4 rows to every device, itself included. `mesh_sources`: A value under 256 is a local row; a value 256 + s * 4 + k is halo slot k from device s.
All inputs are finite; a program needn't handle non-finite values.
Results may differ from a plain program's by a relative error of at most 0.024.
Values may be sent and summed in bfloat16 or wider, within the bound.
No kernel may reach another device: no remote copies, remote signals or barrier semaphores. Data moves between devices by JAX's collectives and lax.ppermute only.
A program may use at most 128 MiB of HBM per device.

v0:
```python
import math
import jax
import jax.numpy as jnp
from jax import lax
from jax.sharding import PartitionSpec as P

EPSILON = 1e-05
HIGHEST = lax.Precision.HIGHEST


def matmul(left, right):
    return jnp.dot(left, right, preferred_element_type=jnp.float32)


def weight_grad(left, right):
    return lax.dot_general(
        left, right, (((0,), (0,)), ((), ())), preferred_element_type=jnp.float32
    )


def input_grad(left, right):
    return lax.dot_general(
        left, right, (((1,), (1,)), ((), ())), preferred_element_type=jnp.float32
    )


def normalize(values):
    center = jnp.mean(values, axis=-1, keepdims=True)
    shifted = values - center
    inverse = lax.rsqrt(jnp.mean(shifted * shifted, axis=-1, keepdims=True) + EPSILON)
    return (shifted * inverse, inverse)


def normalize_back(normed, inverse, upstream):
    first_mean = jnp.mean(upstream, axis=-1, keepdims=True)
    second_mean = jnp.mean(upstream * normed, axis=-1, keepdims=True)
    return inverse * (upstream - first_mean - normed * second_mean)


def swish_slope(values):
    sigma = jax.nn.sigmoid(values)
    return sigma * (1.0 + values * (1.0 - sigma))


def member_table(indices, count_rows, dtype):
    rows_iota = lax.broadcasted_iota(jnp.int32, (count_rows, indices.shape[0]), 0)
    return (rows_iota == indices[None, :]).astype(dtype)


def on_device(
    grid_latent,
    mesh_embed,
    mesh_edges,
    edge_geometry,
    edge_counts,
    edge_sources,
    edge_targets,
    halo_sources,
    mesh_sources,
    mesh_targets,
    grid_weight,
    geometry_weight,
    message_weight,
    mesh_update,
    mesh_output,
    processor,
    cotangent,
):
    width = mesh_embed.shape[1]
    nodes_local = mesh_embed.shape[0]
    peers = lax.axis_size("graph")
    grid_rows = grid_latent[0]
    slots = edge_sources.shape[1]
    capacity = slots // peers
    position = lax.iota(jnp.int32, slots)
    column = position % capacity
    target_peer = position // capacity
    live = column < edge_counts[0][target_peer]
    geometry = edge_geometry[0]
    geometry_term = jnp.einsum(
        "fs,fd->sd", geometry.astype(jnp.float32), geometry_weight, precision=HIGHEST
    )
    grid_proj = matmul(grid_rows, grid_weight)
    messages = jnp.where(
        live[:, None], jax.nn.silu(grid_proj[edge_sources[0]] + geometry_term), 0.0
    ).astype(jnp.bfloat16)
    arrived = lax.all_to_all(messages, "graph", split_axis=0, concat_axis=0, tiled=True)
    hidden_sum = matmul(member_table(edge_targets[0], nodes_local, jnp.bfloat16), arrived).astype(
        jnp.bfloat16
    )
    aggregate = matmul(hidden_sum, message_weight).astype(jnp.bfloat16)
    pre_update = matmul(mesh_embed, mesh_update[:width]) + matmul(aggregate, mesh_update[width:])
    normed_start, inverse_start = normalize(
        matmul(jax.nn.silu(pre_update).astype(jnp.bfloat16), mesh_output)
    )
    nodes = (mesh_embed.astype(jnp.float32) + normed_start).astype(jnp.bfloat16)
    senders = mesh_sources[0]
    receivers = mesh_targets[0]
    halo_index = halo_sources[0]
    extended_rows = nodes_local + halo_index.shape[0]
    recv_table16 = member_table(receivers, nodes_local, jnp.bfloat16)
    edges = mesh_edges
    layers = processor.shape[0]
    stored = []
    for layer_index in range(layers):
        weights = processor[layer_index]
        incoming = lax.all_to_all(
            nodes[halo_index], "graph", split_axis=0, concat_axis=0, tiled=True
        )
        extended = jnp.concatenate([nodes, incoming], 0)
        send_proj = matmul(extended, weights[width : 2 * width])
        recv_proj = matmul(nodes, weights[2 * width : 3 * width])
        pre_edge = matmul(edges, weights[:width]) + send_proj[senders] + recv_proj[receivers]
        hidden_edge = jax.nn.silu(pre_edge).astype(jnp.bfloat16)
        normed_edge, inverse_edge = normalize(matmul(hidden_edge, weights[3 * width : 4 * width]))
        new_edges = (edges.astype(jnp.float32) + normed_edge).astype(jnp.bfloat16)
        summed = matmul(recv_table16, new_edges).astype(jnp.bfloat16)
        pre_node = matmul(nodes, weights[4 * width : 5 * width]) + matmul(
            summed, weights[5 * width : 6 * width]
        )
        hidden_node = jax.nn.silu(pre_node).astype(jnp.bfloat16)
        normed_node, inverse_node = normalize(matmul(hidden_node, weights[6 * width :]))
        new_nodes = (nodes.astype(jnp.float32) + normed_node).astype(jnp.bfloat16)
        stored.append(
            (
                nodes,
                edges,
                pre_edge,
                hidden_edge,
                normed_edge,
                inverse_edge,
                summed,
                pre_node,
                hidden_node,
                normed_node,
                inverse_node,
            )
        )
        nodes, edges = (new_nodes, new_edges)
    scale = 1.0 / math.sqrt(lax.axis_size("dp") * peers * nodes_local)
    grad_nodes = cotangent[0].astype(jnp.float32)
    grad_edges = jnp.zeros(edges.shape, jnp.float32)
    pieces = [None] * layers
    for layer_index in reversed(range(layers)):
        weights = processor[layer_index]
        (
            layer_nodes,
            layer_edges,
            pre_edge,
            hidden_edge,
            normed_edge,
            inverse_edge,
            summed,
            pre_node,
            hidden_node,
            normed_node,
            inverse_node,
        ) = stored[layer_index]
        q_node = normalize_back(normed_node, inverse_node, grad_nodes).astype(jnp.bfloat16)
        grad_node_second = weight_grad(hidden_node, q_node)
        d_node = (input_grad(q_node, weights[6 * width :]) * swish_slope(pre_node)).astype(
            jnp.bfloat16
        )
        grad_node_own = weight_grad(layer_nodes, d_node)
        grad_node_sum = weight_grad(summed, d_node)
        grad_summed = input_grad(d_node, weights[5 * width : 6 * width])
        edge_upstream = grad_edges + grad_summed[receivers]
        q_edge = normalize_back(normed_edge, inverse_edge, edge_upstream).astype(jnp.bfloat16)
        grad_edge_second = weight_grad(hidden_edge, q_edge)
        d_edge = input_grad(q_edge, weights[3 * width : 4 * width]) * swish_slope(pre_edge)
        d_edge16 = d_edge.astype(jnp.bfloat16)
        send_extended = jax.ops.segment_sum(d_edge, senders, num_segments=extended_rows)
        returned = lax.all_to_all(
            send_extended[nodes_local:].astype(jnp.bfloat16),
            "graph",
            split_axis=0,
            concat_axis=0,
            tiled=True,
        ).astype(jnp.float32)
        grad_send = (
            send_extended[:nodes_local]
            + jax.ops.segment_sum(returned, halo_index, num_segments=nodes_local)
        ).astype(jnp.bfloat16)
        grad_recv = jax.ops.segment_sum(d_edge, receivers, num_segments=nodes_local).astype(
            jnp.bfloat16
        )
        partial_value = (
            jnp.concatenate(
                [
                    weight_grad(layer_edges, d_edge16),
                    weight_grad(layer_nodes, grad_send),
                    weight_grad(layer_nodes, grad_recv),
                    grad_edge_second,
                    grad_node_own,
                    grad_node_sum,
                    grad_node_second,
                ],
                0,
            )
            * scale
        )
        grad_edges = edge_upstream + input_grad(d_edge16, weights[:width])
        grad_nodes = (
            grad_nodes
            + input_grad(d_node, weights[4 * width : 5 * width])
            + input_grad(grad_send, weights[width : 2 * width])
            + input_grad(grad_recv, weights[2 * width : 3 * width])
        )
        pieces[layer_index] = lax.psum(partial_value, ("graph", "dp")).astype(jnp.bfloat16)
    gradients = jnp.stack(pieces)
    return (nodes[None], grad_nodes.astype(jnp.bfloat16)[None], gradients)


def solution(mesh):
    in_specs = (
        P("dp", "graph", None),
        P("graph", None),
        P("graph", None),
        P("graph", None, None),
        P("graph", None),
        P("graph", None),
        P("graph", None),
        P("graph", None),
        P("graph", None),
        P("graph", None),
        P(),
        P(),
        P(),
        P(),
        P(),
        P(),
        P("dp", "graph", None),
    )
    out_specs = (P("dp", "graph", None), P("dp", "graph", None), P())
    return jax.shard_map(
        on_device, mesh=mesh, in_specs=in_specs, out_specs=out_specs, check_vma=False
    )
```

profile of v0, /device:TPU:0, one launch (start us, length us, event | category | flops | bytes accessed | tf_op | source)
XLA Modules:
  0.0 500.3 jit_solution(7372707361949194737)
XLA Ops:
  7.6 4.4 compare_select_fusion.4
  15.6 5.3 %all-to-all-start = ((bf16[8,64,512]{2,1,0:T(8,128)(2,1)}), bf16[8,64,512]{2,1,0:T(8,128)(2,1)S(1)}, u32[]{:S(2)}, u32[]{:S(2)}) async-start(bf16[8,64,512]{2,1,0:T(8,128)(2,1)} %bitcast.14), calls=%async_computation | async-start | bytes 1048576 | tf_op jit(solution)/shard_map/all_to_all | solution.py:87
  24.3 6.3 %all-to-all-done = bf16[8,64,512]{2,1,0:T(8,128)(2,1)S(1)} async-done(((bf16[8,64,512]{2,1,0:T(8,128)(2,1)}), bf16[8,64,512]{2,1,0:T(8,128)(2,1)S(1)}, u32[]{:S(2)}, u32[]{:S(2)}) %all-to-all-start) | async-done | bytes 524320 | tf_op jit(solution)/shard_map/all_to_all | solution.py:87
  43.3 4.9 gather_fusion.3
  49.6 5.0 gather_fusion.2
  54.5 4.5 fusion.2
  70.1 4.3 all-to-all-start.2
  76.6 4.9 gather_fusion.6
  82.9 5.0 gather_fusion.5
  87.9 4.1 fusion.1
  103.7 4.9 gather_fusion.7
  126.1 10.6 %scatter_custom_fusion = f32[288,512]{1,0:T(8,128)S(1)} fusion(s32[1536]{0:T(1024)S(1)} %reduce.6, f32[1536,512]{1,0:T(8,128)} %copy-done.31, f32[]{:T(128)} %constant.79.clone.1), kind=kCustom, calls=%fused_computation.193 | custom fusion | flops 786432 | bytes 590336 | tf_op jit(solution)/shard_map/scatter-add | solution.py:172
  137.3 4.2 all-to-all-start.3
  143.1 10.4 %scatter_custom_fusion.2 = f32[256,512]{1,0:T(8,128)S(1)} fusion(s32[1536]{0:T(1024)S(1)} %reduce.3, f32[1536,512]{1,0:T(8,128)} %copy-done.31, f32[]{:T(128)} %constant.79.clone.1), kind=kCustom, calls=%fused_computation.198 | custom fusion | flops 786432 | bytes 524800 | tf_op jit(solution)/shard_map/scatter-add | solution.py:184
  161.0 5.4 %gather_fusion.8 = f32[1536,512]{1,0:T(8,128)} fusion(f32[256,512]{1,0:T(8,128)S(1)} %fusion.54, s32[2048]{0:T(1024)S(1)} %get-tuple-element.31), kind=kCustom, calls=%fused_computation.8 | custom fusion | bytes 6297600 | tf_op jit(solution)/shard_map/gather | solution.py:167
  170.1 5.3 %fusion.143 = (f32[1536]{0:T(1024)S(1)}, f32[1536]{0:T(1024)S(1)}, f32[1536,512]{0,1:T(8,128)S(1)}) fusion(f32[1536]{0:T(1024)S(1)} %add_rsqrt_fusion.1, f32[1536,512]{0,1:T(8,128)S(1)} %copy-done.3, f32[1536]{0:T(1024)S(1)} %broadcast_multiply_fusion.7, f32[1536,512]{0,1:T(8,128)} %copy.29, f32[1536,512]{0,1:T(8,128)} %copy-done.4, ...), kind=kOutput, calls=%fused_computation.263 | convolution fusion | flops 811594752 | bytes 16277504 | tf_op jit(solution)/shard_map/dot_general | solution.py:22
  177.6 4.6 convolution_multiply_fusion
  182.2 10.6 %scatter_custom_fusion.3 = f32[288,512]{1,0:T(8,128)S(1)} fusion(s32[1536]{0:T(1024)S(1)} %reduce.6, f32[1536,512]{1,0:T(8,128)} %convolution_multiply_fusion, f32[]{:T(128)} %constant.79.clone.1), kind=kCustom, calls=%fused_computation.191 | custom fusion | flops 786432 | bytes 590336 | tf_op jit(solution)/shard_map/scatter-add | solution.py:172
  205.6 7.1 %broadcast_multiply_fusion = f32[3584,512]{1,0:T(8,128)} fusion(f32[3584,512]{1,0:T(8,128)} %convolution_dynamic-update-slice_fusion.3), kind=kLoop, calls=%fused_computation.18 | loop fusion | flops 1835008 | bytes 14680064 | tf_op jit(solution)/shard_map/mul | solution.py:188
  213.4 4.2 all-to-all-start.4
  219.0 10.4 %scatter_custom_fusion.5 = f32[256,512]{1,0:T(8,128)S(1)} fusion(s32[1536]{0:T(1024)S(1)} %reduce.3, f32[1536,512]{1,0:T(8,128)} %convolution_multiply_fusion, f32[]{:T(128)} %constant.79.clone.1), kind=kCustom, calls=%fused_computation.196 | custom fusion | flops 786432 | bytes 524800 | tf_op jit(solution)/shard_map/scatter-add | solution.py:184
  243.1 7.0 %broadcast_multiply_fusion.1 = f32[3584,512]{1,0:T(8,128)} fusion(f32[3584,512]{1,0:T(8,128)} %convolution_dynamic-update-slice_fusion.8), kind=kLoop, calls=%fused_computation.19 | loop fusion | flops 1835008 | bytes 14680064 | tf_op jit(solution)/shard_map/mul | solution.py:188
  250.1 243.1 %all-reduce.2 = (bf16[3584,512]{1,0:T(8,128)(2,1)}, bf16[3584,512]{1,0:T(8,128)(2,1)}) all-reduce(f32[3584,512]{1,0:T(8,128)} %broadcast_multiply_fusion, f32[3584,512]{1,0:T(8,128)} %broadcast_multiply_fusion.1), channel_id=1, replica_groups=mesh['graph'=8,'dp'=4] {'graph','dp'}, use_global_device_ids=true, to_apply=%region_25.26 | all-reduce | flops 3670016 | bytes 22020096 | tf_op jit(solution)/shard_map/psum | solution.py:209
  493.2 6.9 %pad_maximum_fusion = bf16[2,3584,512]{2,1,0:T(8,128)(2,1)} fusion(bf16[1,3584,512]{2,1,0:T(8,128)(2,1)} %bitcast.182, bf16[1,3584,512]{2,1,0:T(8,128)(2,1)} %bitcast.183), kind=kLoop, calls=%fused_computation.15 | loop fusion | flops 3670016 | bytes 14680064 | tf_op jit(solution)/shard_map/stack | solution.py:210
  (233 shorter events, 115.0 us)
Async XLA Ops:
  5.2 7.4 %copy-start.57 = (f32[4,512]{1,0:T(4,128)S(1)}, f32[4,512]{1,0:T(4,128)}, u32[]{:S(2)}) copy-start(f32[4,512]{1,0:T(4,128)} %param.28) | copy-start | bytes 24580
  5.2 7.4 %copy-start.58 = (bf16[1,4,512]{2,1,0:T(4,128)(2,1)S(1)}, bf16[1,4,512]{2,1,0:T(4,128)(2,1)}, u32[]{:S(2)}) copy-start(bf16[1,4,512]{2,1,0:T(4,128)(2,1)} %param.20) | copy-start | bytes 12292
  12.6 8.3 %copy-start.54 = (s32[1,1536]{1,0:T(1,128)S(1)}, s32[1,1536]{1,0:T(1,128)}, u32[]{:S(2)}) copy-start(s32[1,1536]{1,0:T(1,128)} %param.25) | copy-start | bytes 18436
  12.6 8.3 %copy-start.55 = (s32[1,1536]{1,0:T(1,128)S(1)}, s32[1,1536]{1,0:T(1,128)}, u32[]{:S(2)}) copy-start(s32[1,1536]{1,0:T(1,128)} %param.26) | copy-start | bytes 18436
  12.7 8.4 %copy-start.32 = (bf16[1,256,512]{2,1,0:T(8,128)(2,1)S(1)}, bf16[1,256,512]{2,1,0:T(8,128)(2,1)}, u32[]{:S(2)}) copy-start(bf16[1,256,512]{2,1,0:T(8,128)(2,1)} %param.33) | copy-start | bytes 786436
  15.6 7.4 %copy-start.42 = (bf16[256,512]{1,0:T(8,128)(2,1)S(1)}, bf16[256,512]{1,0:T(8,128)(2,1)}, u32[]{:S(2)}) copy-start(bf16[256,512]{1,0:T(8,128)(2,1)} %param.18) | copy-start | bytes 786436
  15.6 15.0 %copy-start.59 = (s32[1,512]{1,0:T(1,128)S(1)}, s32[1,512]{1,0:T(1,128)}, u32[]{:S(2)}) copy-start(s32[1,512]{1,0:T(1,128)} %param.23) | copy-start | bytes 6148
  15.6 15.0 %all-to-all-start = ((bf16[8,64,512]{2,1,0:T(8,128)(2,1)}), bf16[8,64,512]{2,1,0:T(8,128)(2,1)S(1)}, u32[]{:S(2)}, u32[]{:S(2)}) async-start(bf16[8,64,512]{2,1,0:T(8,128)(2,1)} %bitcast.14), calls=%async_computation | async-start | bytes 1048576 | tf_op jit(solution)/shard_map/all_to_all | solution.py:87
  36.5 11.7 %all-to-all-start.1 = ((bf16[8,4,512]{2,1,0:T(4,128)(2,1)}), bf16[8,4,512]{2,1,0:T(4,128)(2,1)S(1)}, u32[]{:S(2)}, u32[]{:S(2)}) async-start(bf16[8,4,512]{2,1,0:T(4,128)(2,1)} %all_to_all.39), calls=%async_computation.1 | async-start | bytes 65536 | tf_op jit(solution)/shard_map/all_to_all | solution.py:107
  67.1 14.4 %copy-start.9 = (f32[256,512]{1,0:T(8,128)}, f32[256,512]{1,0:T(8,128)S(1)}, u32[]{:S(2)}) copy-start(f32[256,512]{1,0:T(8,128)S(1)} %get-tuple-element.24) | copy-start | bytes 1572868
  67.5 32.3 %copy-start.7 = (bf16[256,512]{1,0:T(8,128)(2,1)}, bf16[256,512]{1,0:T(8,128)(2,1)S(1)}, u32[]{:S(2)}) copy-start(bf16[256,512]{1,0:T(8,128)(2,1)S(1)} %add_convert_fusion.6) | copy-start | bytes 786436
  70.1 11.4 %all-to-all-start.2 = ((bf16[8,4,512]{2,1,0:T(4,128)(2,1)}), bf16[8,4,512]{2,1,0:T(4,128)(2,1)S(1)}, u32[]{:S(2)}, u32[]{:S(2)}) async-start(bf16[8,4,512]{2,1,0:T(4,128)(2,1)} %all_to_all.42), calls=%async_computation.2 | async-start | bytes 65536 | tf_op jit(solution)/shard_map/all_to_all | solution.py:107
  94.6 7.6 %copy-start.5 = (f32[1536,512]{0,1:T(8,128)}, f32[1536,512]{0,1:T(8,128)S(1)}, u32[]{:S(2)}) copy-start(f32[1536,512]{0,1:T(8,128)S(1)} %get-tuple-element.26) | copy-start | bytes 9437188
  111.0 11.4 %copy-start.4 = (f32[1536,512]{0,1:T(8,128)}, f32[1536,512]{0,1:T(8,128)S(1)}, u32[]{:S(2)}) copy-start(f32[1536,512]{0,1:T(8,128)S(1)} %copy.26) | copy-start | bytes 9437188
  126.1 27.5 %copy-start.56 = (s32[1,32]{1,0:T(1,128)S(1)}, s32[1,32]{1,0:T(1,128)}, u32[]{:S(2)}) copy-start(s32[1,32]{1,0:T(1,128)} %param.24) | copy-start | bytes 388
  137.3 16.2 %all-to-all-start.3 = ((bf16[8,4,512]{2,1,0:T(4,128)(2,1)}), bf16[8,4,512]{2,1,0:T(4,128)(2,1)S(1)}, u32[]{:S(2)}, u32[]{:S(2)}) async-start(bf16[8,4,512]{2,1,0:T(4,128)(2,1)} %all_to_all.45), calls=%async_computation.3 | async-start | bytes 65536 | tf_op jit(solution)/shard_map/all_to_all | solution.py:173
  141.5 14.7 %copy-start.10 = (f32[256,512]{1,0:T(8,128)S(1)}, f32[256,512]{1,0:T(8,128)}, u32[]{:S(2)}) copy-start(f32[256,512]{1,0:T(8,128)} %copy-done.9) | copy-start | bytes 1572868
  177.6 15.2 %copy-start.13 = (bf16[1536,512]{1,0:T(8,128)(2,1)S(1)}, bf16[1536,512]{1,0:T(8,128)(2,1)}, u32[]{:S(2)}) copy-start(bf16[1536,512]{1,0:T(8,128)(2,1)} %param.19) | copy-start | bytes 4718596
  192.8 5.4 %copy-start.20 = (f32[256,512]{1,0:T(8,128)S(1)}, f32[256,512]{1,0:T(8,128)}, u32[]{:S(2)}) copy-start(f32[256,512]{1,0:T(8,128)} %copy-done.19) | copy-start | bytes 1572868
  192.8 6.7 %copy-start.39 = (bf16[1536,512]{0,1:T(8,128)(2,1)S(1)}, bf16[1536,512]{0,1:T(8,128)(2,1)}, u32[]{:S(2)}) copy-start(bf16[1536,512]{0,1:T(8,128)(2,1)} %copy-done.38) | copy-start | bytes 4718596
  205.6 12.0 %copy-start.18 = (f32[256,512]{1,0:T(8,128)S(1)}, f32[256,512]{1,0:T(8,128)}, u32[]{:S(2)}) copy-start(f32[256,512]{1,0:T(8,128)} %copy-done.17) | copy-start | bytes 1572868
  205.6 12.0 %copy-start.22 = (bf16[256,512]{1,0:T(8,128)(2,1)S(1)}, bf16[256,512]{1,0:T(8,128)(2,1)}, u32[]{:S(2)}) copy-start(bf16[256,512]{1,0:T(8,128)(2,1)} %copy-done.21) | copy-start | bytes 786436
  213.4 16.0 %all-to-all-start.4 = ((bf16[8,4,512]{2,1,0:T(4,128)(2,1)}), bf16[8,4,512]{2,1,0:T(4,128)(2,1)S(1)}, u32[]{:S(2)}, u32[]{:S(2)}) async-start(bf16[8,4,512]{2,1,0:T(4,128)(2,1)} %all_to_all.47), calls=%async_computation.4 | async-start | bytes 65536 | tf_op jit(solution)/shard_map/all_to_all | solution.py:173
  493.2 6.9 %copy-start.1 = (bf16[512,512]{1,0:T(8,128)(2,1)S(1)}, bf16[512,512]{1,0:T(8,128)(2,1)}, u32[]{:S(2)}) copy-start(bf16[512,512]{1,0:T(8,128)(2,1)} %param.27) | copy-start | bytes 1572868
  (41 other events, 137.7 us)
where the time goes:
time: 509 us; the launch traced here: 500 us
  blocking collectives  243 us (48%)
  matrix products  93.5 us (18%)
  other arithmetic  82.9 us (16%)
  local copies, waits for them, and re-layouts  51.2 us (10%)
  starting transfers between devices  21.4 us (4%)
  waiting for transfers between devices  6.35 us (1%)
    psum x1, blocking collectives, on_device(): lax.psum(partial_value, ('graph', 'dp')).astype(jnp.bfloat16)  243 us
    dot_general x20, matrix products, matmul(): return jnp.dot(left, right, preferred_element_type=jnp.float32)  38 us
    dot_general x13, matrix products, input_grad(): lax.dot_general(left, right, (((1,), (1,)), ((), ())), preferred_element_...  29.1 us
    dot_general x14, matrix products, weight_grad(): lax.dot_general(left, right, (((0,), (0,)), ((), ())), preferred_element_...  23.4 us
    scatter-add x2, other arithmetic, on_device(): jax.ops.segment_sum(d_edge, senders, num_segments=extended_rows)  21.2 us
    scatter-add x2, other arithmetic, on_device(): jax.ops.segment_sum(d_edge, receivers, num_segments=nodes_local)  20.7 us
    gather x4, local copies, waits for them, and re-layouts, on_device(): edge_upstream = grad_edges + grad_summed[receivers]  16.3 us
    mul x2, other arithmetic, on_device(): jnp.concatenate([weight_grad(layer_edges, d_edge16), weight_grad(layer_no...  14.1 us
  transfers between devices with their start and end apart: 5, of which 1 were waited for; matrix products, arithmetic and copies ran while one was open for 8% of the time, Pallas kernels for 0%

commit v1 on v0

--- a/solution.py
+++ b/solution.py
@@ -6,6 +6,22 @@
 
 EPSILON = 1e-05
 HIGHEST = lax.Precision.HIGHEST
+
+
+def pair_streams(raw, d_out, array_in):
+    tall = raw.shape
+    x_new = raw.reshape(*tall[:d_out], array_in, tall[d_out] // array_in, *tall[d_out + 1 :])
+    local_now = jnp.moveaxis(x_new, d_out, 0)
+    return local_now
+
+
+def levels_all_review(z_in, dim_i):
+    z_in = jnp.moveaxis(z_in, 0, dim_i)
+    b_next = z_in.shape
+    frame_out = z_in.reshape(
+        *b_next[:dim_i], b_next[dim_i] * b_next[dim_i + 1], *b_next[dim_i + 2 :]
+    )
+    return frame_out
 
 
 def matmul(left, right):
@@ -84,7 +100,18 @@
     messages = jnp.where(
         live[:, None], jax.nn.silu(grid_proj[edge_sources[0]] + geometry_term), 0.0
     ).astype(jnp.bfloat16)
-    arrived = lax.all_to_all(messages, "graph", split_axis=0, concat_axis=0, tiled=True)
+    s_next = lax.axis_size("graph")
+    main = lax.axis_index("graph")
+    high, f_now = (s_next, main)
+    res = pair_streams(messages, 0, high)
+    by_place = [res[f_now]]
+    for rr in tuple(range(1, high)):
+        new = res[f_now ^ rr]
+        piece_next = lax.ppermute(new, "graph", [(kk, kk ^ rr) for kk in range(high)])
+        by_place.append(piece_next)
+    v_now = jnp.stack(by_place)
+    res = v_now[f_now ^ jnp.arange(high)]
+    arrived = levels_all_review(res, 0)
     hidden_sum = matmul(member_table(edge_targets[0], nodes_local, jnp.bfloat16), arrived).astype(
         jnp.bfloat16
     )

time: 509 us -> 518 us (1.018)
  local copies, waits for them, and re-layouts: 51.2 us -> 57.5 us
    ppermute x0 -> x7, starting transfers between devices: none -> 8.37 us  [on_device(): lax.ppermute(new, 'graph', [(kk, kk ^ rr) for kk in range(high)])]
    all_to_all x1 -> x0, waiting for transfers between devices: 6.34 us -> none  [on_device(): lax.all_to_all(messages, 'graph', split_axis=0, concat_axis=0, tiled=True)]
    ppermute x0 -> x7, waiting for transfers between devices: none -> 5.4 us  [on_device(): lax.ppermute(new, 'graph', [(kk, kk ^ rr) for kk in range(high)])]
    all_to_all x1 -> x0, starting transfers between devices: 5.33 us -> none  [on_device(): lax.all_to_all(messages, 'graph', split_axis=0, concat_axis=0, tiled=True)]
    unnamed x121 -> x129, local copies, waits for them, and re-layouts: 7.25 us -> 10.6 us
  transfers between devices with their start and end apart: 5 -> 11, of which waited for: 1 -> 2; matrix products, arithmetic and copies ran while one was open for 8% -> 9% of each run, Pallas kernels for 0% -> 0%
where the time goes in v1:
time: 518 us; the launch traced here: 508 us
  blocking collectives  243 us (47%)
  matrix products  92.8 us (18%)
  other arithmetic  82.2 us (16%)
  local copies, waits for them, and re-layouts  57.5 us (11%)
  starting transfers between devices  25.1 us (5%)
  waiting for transfers between devices  5.42 us (1%)
    psum x1, blocking collectives, on_device(): lax.psum(partial_value, ('graph', 'dp')).astype(jnp.bfloat16)  243 us
    dot_general x20, matrix products, matmul(): return jnp.dot(left, right, preferred_element_type=jnp.float32)  38.2 us
    dot_general x13, matrix products, input_grad(): lax.dot_general(left, right, (((1,), (1,)), ((), ())), preferred_element_...  29.1 us
    dot_general x14, matrix products, weight_grad(): lax.dot_general(left, right, (((0,), (0,)), ((), ())), preferred_element_...  23.4 us
    scatter-add x2, other arithmetic, on_device(): jax.ops.segment_sum(d_edge, senders, num_segments=extended_rows)  21.2 us
    scatter-add x2, other arithmetic, on_device(): jax.ops.segment_sum(d_edge, receivers, num_segments=nodes_local)  20.7 us
    gather x4, local copies, waits for them, and re-layouts, on_device(): edge_upstream = grad_edges + grad_summed[receivers]  16.3 us
    mul x2, other arithmetic, on_device(): jnp.concatenate([weight_grad(layer_edges, d_edge16), weight_grad(layer_no...  14.1 us
  transfers between devices with their start and end apart: 11, of which 2 were waited for; matrix products, arithmetic and copies ran while one was open for 9% of the time, Pallas kernels for 0%

profile of v1, /device:TPU:0, one launch (start us, length us, event | category | flops | bytes accessed | tf_op | source)
XLA Modules:
  0.0 508.3 jit_solution(5928721985930046746)
XLA Ops:
  2.3 5.1 %compare_select_fusion.2 = (s32[512,1]{0,1:T(1,128)S(1)}, s32[512,1]{0,1:T(1,128)S(1)}) fusion(s32[1,512]{1,0:T(1,128)} %param.22, s32[]{:T(128)} %bitcast.8, s32[]{:T(128)} %bitcast.7, s32[]{:T(128)} %bitcast.6, s32[]{:T(128)} %bitcast.5, s32[]{:T(128)} %bitcast.4, s32[]{:T(128)} %bitcast.3, s32[]{:T(128)} %bitcast.2), kind=kLoop, calls=%fused_computation.230 | loop fusion | flops 13312 | bytes 6172 | tf_op jit(solution)/shard_map/select_n | solution.py:101
  43.8 4.0 all-to-all-start
  51.2 4.9 gather_fusion.4
  57.5 5.0 gather_fusion.3
  62.5 4.5 fusion.2
  78.0 4.4 all-to-all-start.1
  84.6 4.9 gather_fusion.7
  90.9 5.0 gather_fusion.6
  95.9 4.1 fusion.1
  111.7 4.9 gather_fusion.8
  134.1 10.6 %scatter_custom_fusion = f32[288,512]{1,0:T(8,128)S(1)} fusion(s32[1536]{0:T(1024)S(1)} %reduce.6, f32[1536,512]{1,0:T(8,128)} %copy-done.31, f32[]{:T(128)} %constant.94.clone.1), kind=kCustom, calls=%fused_computation.194 | custom fusion | flops 786432 | bytes 590336 | tf_op jit(solution)/shard_map/scatter-add | solution.py:199
  145.3 4.2 all-to-all-start.2
  151.1 10.4 %scatter_custom_fusion.2 = f32[256,512]{1,0:T(8,128)S(1)} fusion(s32[1536]{0:T(1024)S(1)} %reduce.3, f32[1536,512]{1,0:T(8,128)} %copy-done.31, f32[]{:T(128)} %constant.94.clone.1), kind=kCustom, calls=%fused_computation.199 | custom fusion | flops 786432 | bytes 524800 | tf_op jit(solution)/shard_map/scatter-add | solution.py:211
  169.0 5.4 %gather_fusion.9 = f32[1536,512]{1,0:T(8,128)} fusion(f32[256,512]{1,0:T(8,128)S(1)} %fusion.54, s32[2048]{0:T(1024)S(1)} %get-tuple-element.41), kind=kCustom, calls=%fused_computation.9 | custom fusion | bytes 6297600 | tf_op jit(solution)/shard_map/gather | solution.py:194
  178.1 5.3 %fusion.144 = (f32[1536]{0:T(1024)S(1)}, f32[1536]{0:T(1024)S(1)}, f32[1536,512]{0,1:T(8,128)S(1)}) fusion(f32[1536]{0:T(1024)S(1)} %add_rsqrt_fusion.1, f32[1536,512]{0,1:T(8,128)S(1)} %copy-done.3, f32[1536]{0:T(1024)S(1)} %broadcast_multiply_fusion.7, f32[1536,512]{0,1:T(8,128)} %copy.29, f32[1536,512]{0,1:T(8,128)} %copy-done.4, ...), kind=kOutput, calls=%fused_computation.282 | convolution fusion | flops 811594752 | bytes 16277504 | tf_op jit(solution)/shard_map/dot_general | solution.py:38
  185.5 4.6 convolution_multiply_fusion
  190.1 10.6 %scatter_custom_fusion.3 = f32[288,512]{1,0:T(8,128)S(1)} fusion(s32[1536]{0:T(1024)S(1)} %reduce.6, f32[1536,512]{1,0:T(8,128)} %convolution_multiply_fusion, f32[]{:T(128)} %constant.94.clone.1), kind=kCustom, calls=%fused_computation.192 | custom fusion | flops 786432 | bytes 590336 | tf_op jit(solution)/shard_map/scatter-add | solution.py:199
  200.7 4.1 fusion.12
  213.6 7.1 %broadcast_multiply_fusion = f32[3584,512]{1,0:T(8,128)} fusion(f32[3584,512]{1,0:T(8,128)} %convolution_dynamic-update-slice_fusion.3), kind=kLoop, calls=%fused_computation.19 | loop fusion | flops 1835008 | bytes 14680064 | tf_op jit(solution)/shard_map/mul | solution.py:215
  221.4 4.2 all-to-all-start.3
  226.9 10.4 %scatter_custom_fusion.5 = f32[256,512]{1,0:T(8,128)S(1)} fusion(s32[1536]{0:T(1024)S(1)} %reduce.3, f32[1536,512]{1,0:T(8,128)} %convolution_multiply_fusion, f32[]{:T(128)} %constant.94.clone.1), kind=kCustom, calls=%fused_computation.197 | custom fusion | flops 786432 | bytes 524800 | tf_op jit(solution)/shard_map/scatter-add | solution.py:211
  251.1 7.0 %broadcast_multiply_fusion.1 = f32[3584,512]{1,0:T(8,128)} fusion(f32[3584,512]{1,0:T(8,128)} %convolution_dynamic-update-slice_fusion.8), kind=kLoop, calls=%fused_computation.20 | loop fusion | flops 1835008 | bytes 14680064 | tf_op jit(solution)/shard_map/mul | solution.py:215
  258.1 243.1 %all-reduce.2 = (bf16[3584,512]{1,0:T(8,128)(2,1)}, bf16[3584,512]{1,0:T(8,128)(2,1)}) all-reduce(f32[3584,512]{1,0:T(8,128)} %broadcast_multiply_fusion, f32[3584,512]{1,0:T(8,128)} %broadcast_multiply_fusion.1), channel_id=1, replica_groups=mesh['graph'=8,'dp'=4] {'graph','dp'}, use_global_device_ids=true, to_apply=%region_25.26 | all-reduce | flops 3670016 | bytes 22020096 | tf_op jit(solution)/shard_map/psum | solution.py:236
  501.1 6.9 %pad_maximum_fusion = bf16[2,3584,512]{2,1,0:T(8,128)(2,1)} fusion(bf16[1,3584,512]{2,1,0:T(8,128)(2,1)} %bitcast.212, bf16[1,3584,512]{2,1,0:T(8,128)(2,1)} %bitcast.213), kind=kLoop, calls=%fused_computation.16 | loop fusion | flops 3670016 | bytes 14680064 | tf_op jit(solution)/shard_map/stack | solution.py:237
  (258 shorter events, 125.7 us)
Async XLA Ops:
  12.0 8.7 %copy-start.55 = (s32[1,1536]{1,0:T(1,128)S(1)}, s32[1,1536]{1,0:T(1,128)}, u32[]{:S(2)}) copy-start(s32[1,1536]{1,0:T(1,128)} %param.25) | copy-start | bytes 18436
  12.0 8.7 %copy-start.56 = (s32[1,1536]{1,0:T(1,128)S(1)}, s32[1,1536]{1,0:T(1,128)}, u32[]{:S(2)}) copy-start(s32[1,1536]{1,0:T(1,128)} %param.26) | copy-start | bytes 18436
  12.0 8.8 %copy-start.57 = (s32[1,32]{1,0:T(1,128)S(1)}, s32[1,32]{1,0:T(1,128)}, u32[]{:S(2)}) copy-start(s32[1,32]{1,0:T(1,128)} %param.24) | copy-start | bytes 388
  12.1 8.8 %copy-start.32 = (bf16[1,256,512]{2,1,0:T(8,128)(2,1)S(1)}, bf16[1,256,512]{2,1,0:T(8,128)(2,1)}, u32[]{:S(2)}) copy-start(bf16[1,256,512]{2,1,0:T(8,128)(2,1)} %param.33) | copy-start | bytes 786436
  14.9 13.9 %copy-start.54 = (bf16[64,512]{1,0:T(8,128)(2,1)S(1)}, bf16[64,512]{1,0:T(8,128)(2,1)}, u32[]{:S(2)}) copy-start(bf16[64,512]{1,0:T(8,128)(2,1)} %get-tuple-element.15) | copy-start | bytes 196612
  14.9 20.6 %collective-permute-start.6 = (bf16[64,512]{1,0:T(8,128)(2,1)S(1)}, bf16[64,512]{1,0:T(8,128)(2,1)}, u32[]{:S(2)}, u32[]{:S(2)}) collective-permute-start(bf16[64,512]{1,0:T(8,128)(2,1)S(1)} %get-tuple-element.11), channel_id=1, source_target_pairs={{0,28},{4,24},{8,20},{12,16},{16,12},{20,8},{24,4},{28,0},{1,29},{... | collective-permute-start | bytes 196616 | tf_op jit(solution)/shard_map/ppermute | solution.py:110
  18.3 16.4 %collective-permute-start.5 = (bf16[64,512]{1,0:T(8,128)(2,1)S(1)}, bf16[64,512]{1,0:T(8,128)(2,1)}, u32[]{:S(2)}, u32[]{:S(2)}) collective-permute-start(bf16[64,512]{1,0:T(8,128)(2,1)S(1)} %get-tuple-element.12), channel_id=1, source_target_pairs={{0,24},{4,28},{8,16},{12,20},{16,8},{20,12},{24,0},{28,4},{1,25},{... | collective-permute-start | bytes 196616 | tf_op jit(solution)/shard_map/ppermute | solution.py:110
  18.8 15.0 %collective-permute-start.4 = (bf16[64,512]{1,0:T(8,128)(2,1)S(1)}, bf16[64,512]{1,0:T(8,128)(2,1)}, u32[]{:S(2)}, u32[]{:S(2)}) collective-permute-start(bf16[64,512]{1,0:T(8,128)(2,1)S(1)} %get-tuple-element.13), channel_id=1, source_target_pairs={{0,20},{4,16},{8,28},{12,24},{16,4},{20,0},{24,12},{28,8},{1,21},{... | collective-permute-start | bytes 196616 | tf_op jit(solution)/shard_map/ppermute | solution.py:110
  20.3 12.7 %collective-permute-start.3 = (bf16[64,512]{1,0:T(8,128)(2,1)S(1)}, bf16[64,512]{1,0:T(8,128)(2,1)}, u32[]{:S(2)}, u32[]{:S(2)}) collective-permute-start(bf16[64,512]{1,0:T(8,128)(2,1)S(1)} %get-tuple-element.14), channel_id=1, source_target_pairs={{0,16},{4,20},{8,24},{12,28},{16,0},{20,4},{24,8},{28,12},{1,17},{... | collective-permute-start | bytes 196616 | tf_op jit(solution)/shard_map/ppermute | solution.py:110
  20.6 3.5 collective-permute-start
  21.0 16.7 %copy-start.60 = (s32[1,512]{1,0:T(1,128)S(1)}, s32[1,512]{1,0:T(1,128)}, u32[]{:S(2)}) copy-start(s32[1,512]{1,0:T(1,128)} %param.23) | copy-start | bytes 6148
  24.1 4.7 collective-permute-start.1
  28.8 4.2 collective-permute-start.2
  43.8 12.4 %all-to-all-start = ((bf16[8,4,512]{2,1,0:T(4,128)(2,1)}), bf16[8,4,512]{2,1,0:T(4,128)(2,1)S(1)}, u32[]{:S(2)}, u32[]{:S(2)}) async-start(bf16[8,4,512]{2,1,0:T(4,128)(2,1)} %all_to_all.28), calls=%async_computation | async-start | bytes 65536 | tf_op jit(solution)/shard_map/all_to_all | solution.py:134
  75.0 14.5 %copy-start.9 = (f32[256,512]{1,0:T(8,128)}, f32[256,512]{1,0:T(8,128)S(1)}, u32[]{:S(2)}) copy-start(f32[256,512]{1,0:T(8,128)S(1)} %get-tuple-element.32) | copy-start | bytes 1572868
  75.4 32.3 %copy-start.7 = (bf16[256,512]{1,0:T(8,128)(2,1)}, bf16[256,512]{1,0:T(8,128)(2,1)S(1)}, u32[]{:S(2)}) copy-start(bf16[256,512]{1,0:T(8,128)(2,1)S(1)} %add_convert_fusion.6) | copy-start | bytes 786436
  78.0 11.5 %all-to-all-start.1 = ((bf16[8,4,512]{2,1,0:T(4,128)(2,1)}), bf16[8,4,512]{2,1,0:T(4,128)(2,1)S(1)}, u32[]{:S(2)}, u32[]{:S(2)}) async-start(bf16[8,4,512]{2,1,0:T(4,128)(2,1)} %all_to_all.31), calls=%async_computation.1 | async-start | bytes 65536 | tf_op jit(solution)/shard_map/all_to_all | solution.py:134
  119.0 11.4 %copy-start.4 = (f32[1536,512]{0,1:T(8,128)}, f32[1536,512]{0,1:T(8,128)S(1)}, u32[]{:S(2)}) copy-start(f32[1536,512]{0,1:T(8,128)S(1)} %copy.26) | copy-start | bytes 9437188
  145.3 16.2 %all-to-all-start.2 = ((bf16[8,4,512]{2,1,0:T(4,128)(2,1)}), bf16[8,4,512]{2,1,0:T(4,128)(2,1)S(1)}, u32[]{:S(2)}, u32[]{:S(2)}) async-start(bf16[8,4,512]{2,1,0:T(4,128)(2,1)} %all_to_all.34), calls=%async_computation.2 | async-start | bytes 65536 | tf_op jit(solution)/shard_map/all_to_all | solution.py:200
  149.5 14.7 %copy-start.10 = (f32[256,512]{1,0:T(8,128)S(1)}, f32[256,512]{1,0:T(8,128)}, u32[]{:S(2)}) copy-start(f32[256,512]{1,0:T(8,128)} %copy-done.9) | copy-start | bytes 1572868
  185.5 15.2 %copy-start.13 = (bf16[1536,512]{1,0:T(8,128)(2,1)S(1)}, bf16[1536,512]{1,0:T(8,128)(2,1)}, u32[]{:S(2)}) copy-start(bf16[1536,512]{1,0:T(8,128)(2,1)} %param.19) | copy-start | bytes 4718596
  213.6 12.0 %copy-start.18 = (f32[256,512]{1,0:T(8,128)S(1)}, f32[256,512]{1,0:T(8,128)}, u32[]{:S(2)}) copy-start(f32[256,512]{1,0:T(8,128)} %copy-done.17) | copy-start | bytes 1572868
  213.6 12.0 %copy-start.22 = (bf16[256,512]{1,0:T(8,128)(2,1)S(1)}, bf16[256,512]{1,0:T(8,128)(2,1)}, u32[]{:S(2)}) copy-start(bf16[256,512]{1,0:T(8,128)(2,1)} %copy-done.21) | copy-start | bytes 786436
  221.4 16.0 %all-to-all-start.3 = ((bf16[8,4,512]{2,1,0:T(4,128)(2,1)}), bf16[8,4,512]{2,1,0:T(4,128)(2,1)S(1)}, u32[]{:S(2)}, u32[]{:S(2)}) async-start(bf16[8,4,512]{2,1,0:T(4,128)(2,1)} %all_to_all.36), calls=%async_computation.3 | async-start | bytes 65536 | tf_op jit(solution)/shard_map/all_to_all | solution.py:200
  (48 other events, 182.6 us)
